TPU v7x, 256 devices: a whole 4x4x8 slice. The times are simulated.
256 devices in a mesh: view: 32 (over y, x, core), strip: 8 (over z).
Axes of the slice: x: 4, y: 4, z: 8, core: 2. Of those that a mesh axis runs over, the one named last changes fastest.
Arguments:
- tokens: bfloat16 [32, 1024, 1536], P('view', 'strip'), may hold values from -48 to 48
- source_ids: int32 [32, 8, 5], replicated, may hold values from 0 to 255, as said below
- source_count: int32 [32, 8], replicated, may hold values from 2 to 5, as said below
- self_query: bfloat16 [1536, 1536], P(None, 'strip'), may hold values from -24 to 24
- self_key: bfloat16 [1536, 1536], P(None, 'strip'), may hold values from -24 to 24
- self_value: bfloat16 [1536, 1536], P(None, 'strip'), may hold values from -0.15625 to 0.15625
- self_out: bfloat16 [1536, 1536], P('strip'), may hold values from -1.1953125 to 1.1953125
- cross_query: bfloat16 [1536, 1536], P(None, 'strip'), may hold values from -24 to 24
- cross_key: bfloat16 [1536, 1536], P(None, 'strip'), may hold values from -24 to 24
- cross_value: bfloat16 [1536, 1536], P(None, 'strip'), may hold values from -0.15625 to 0.15625
- cross_out: bfloat16 [1536, 1536], P('strip'), may hold values from -1.1953125 to 1.1953125
- mlp_up: bfloat16 [1536, 6144], P(None, 'strip'), may hold values from -0.15625 to 0.15625
- mlp_down: bfloat16 [6144, 1536], P('strip'), may hold values from -0.078125 to 0.078125
Outputs:
- mixed: bfloat16 [32, 1024, 1536], P('view', 'strip')
Inputs may be any that keep to these rules, and one draw needn't show every extreme that they name: `source_ids`: entry k of strip s of view v names a strip of another view than v; entries with k >= source_count[v, s] are unused. Among all 40 entries of one destination view, used or not, each other view is named at most 2 times, and some view exactly 2 times. `source_count`: every view has a strip with all 5 entries in use.
All inputs are finite; a program needn't handle non-finite values.
Results may differ from a plain program's by a relative error of at most 0.015.
Values may be sent and summed in bfloat16 or wider, within the bound.
No kernel may reach another device: no remote copies, remote signals or barrier semaphores. Data moves between devices by JAX's collectives and lax.ppermute only.
A program may use at most 128 MiB of HBM per device.

v0:
```python
import math
import jax
import jax.numpy as jnp
from jax import lax
from jax.sharding import PartitionSpec as P

HEAD_DIM = 64
SLOTS = 5


def rms_rows(values_in):
    widened = values_in.astype(jnp.float32)
    scaled = widened * lax.rsqrt(jnp.mean(widened * widened, axis=-1, keepdims=True) + 1e-06)
    return scaled.astype(jnp.bfloat16)


def attend_heads(query_heads, key_heads, value_heads, key_mask):
    scale = 1.0 / math.sqrt(HEAD_DIM)
    scores = (
        jnp.einsum("qhe,khe->hqk", query_heads, key_heads, preferred_element_type=jnp.float32)
        * scale
    )
    scores = jnp.where(key_mask[None, None, :], scores, -1e30)
    weights = jax.nn.softmax(scores, axis=-1).astype(jnp.bfloat16)
    mixed_heads = jnp.einsum(
        "hqk,khe->qhe", weights, value_heads, preferred_element_type=jnp.float32
    )
    return mixed_heads.reshape(mixed_heads.shape[0], -1).astype(jnp.bfloat16)


def branch_term(mixed_rows, weight):
    return jnp.dot(mixed_rows, weight, preferred_element_type=jnp.float32)


def per_device(
    tokens,
    source_ids,
    source_count,
    self_query,
    self_key,
    self_value,
    self_out,
    cross_query,
    cross_key,
    cross_value,
    cross_out,
    mlp_up,
    mlp_down,
):
    n_view = lax.axis_size("view")
    n_strip = lax.axis_size("strip")
    my_view = lax.axis_index("view")
    strip_rows = tokens.shape[1]
    head_cols = self_query.shape[1]
    heads_here = head_cols // HEAD_DIM
    capacity = (n_strip * SLOTS + n_view - 2) // (n_view - 1)
    normed = rms_rows(tokens[0])
    stacked = jnp.concatenate(
        [self_query, self_key, self_value, cross_query, cross_key, cross_value, mlp_up], 1
    )
    split_at = 6 * head_cols
    product = jnp.dot(
        lax.all_gather(normed, "strip", axis=0, tiled=True),
        stacked,
        preferred_element_type=jnp.float32,
    )
    projected = jnp.concatenate(
        [product[:, :split_at], jax.nn.gelu(product[:, split_at:])], 1
    ).astype(jnp.bfloat16)
    total_rows = projected.shape[0]
    flat_ids = source_ids.reshape(n_view, -1)
    source_view = flat_ids // n_strip
    source_strip = flat_ids % n_strip
    entry_count = flat_ids.shape[1]
    entry_order = jnp.arange(entry_count, dtype=jnp.int32)
    earlier = entry_order[None, :] < entry_order[:, None]
    same_view = source_view[:, :, None] == source_view[:, None, :]
    slot_rank = jnp.sum(jnp.logical_and(same_view, earlier[None]), axis=2)
    slot_index = jnp.arange(capacity, dtype=jnp.int32)
    slot_match = jnp.logical_and(
        (source_view == my_view)[:, :, None], slot_rank[:, :, None] == slot_index[None, None, :]
    )
    strip_table = jnp.sum(jnp.where(slot_match, source_strip[:, :, None], 0), axis=1)
    cross_pairs = projected[:, 4 * head_cols : 6 * head_cols].reshape(
        n_strip, strip_rows, 2 * head_cols
    )
    outgoing = cross_pairs[strip_table]
    received = lax.all_to_all(outgoing, "view", split_axis=0, concat_axis=0, tiled=True)

    def head_block(column_block):
        return projected[:, column_block * head_cols : (column_block + 1) * head_cols].reshape(
            total_rows, heads_here, HEAD_DIM
        )

    self_mix = attend_heads(
        head_block(0), head_block(1), head_block(2), jnp.ones((total_rows,), dtype=bool)
    )
    hidden = projected[:, split_at:]
    my_source = lax.dynamic_index_in_dim(source_view, my_view, 0, keepdims=False)
    my_rank = lax.dynamic_index_in_dim(slot_rank, my_view, 0, keepdims=False)
    picked = received.reshape(n_view * capacity, strip_rows, 2 * head_cols)[
        my_source * capacity + my_rank
    ]
    picked = picked.reshape(n_strip, SLOTS * strip_rows, 2 * head_cols)
    my_count = lax.dynamic_index_in_dim(source_count, my_view, 0, keepdims=False)
    key_valid = jnp.repeat(
        jnp.arange(SLOTS, dtype=jnp.int32)[None, :] < my_count[:, None], strip_rows, axis=1
    )
    cross_heads = projected[:, 3 * head_cols : 4 * head_cols].reshape(
        n_strip, strip_rows, heads_here, HEAD_DIM
    )
    picked_keys = picked[:, :, :head_cols].reshape(
        n_strip, SLOTS * strip_rows, heads_here, HEAD_DIM
    )
    picked_values = picked[:, :, head_cols:].reshape(
        n_strip, SLOTS * strip_rows, heads_here, HEAD_DIM
    )
    cross_mix = jax.vmap(attend_heads)(cross_heads, picked_keys, picked_values, key_valid).reshape(
        total_rows, head_cols
    )
    early_part = lax.psum_scatter(
        (branch_term(self_mix, self_out) + branch_term(hidden, mlp_down)).astype(jnp.bfloat16),
        "strip",
        scatter_dimension=0,
        tiled=True,
    ).astype(jnp.float32)
    cross_part = lax.psum_scatter(
        branch_term(cross_mix, cross_out).astype(jnp.bfloat16),
        "strip",
        scatter_dimension=0,
        tiled=True,
    ).astype(jnp.float32)
    summed = early_part + cross_part
    return (tokens[0].astype(jnp.float32) + summed).astype(jnp.bfloat16)[None]


def solution(mesh):
    in_specs = (
        P("view", "strip", None),
        P(),
        P(),
        P(None, "strip"),
        P(None, "strip"),
        P(None, "strip"),
        P("strip", None),
        P(None, "strip"),
        P(None, "strip"),
        P(None, "strip"),
        P("strip", None),
        P(None, "strip"),
        P("strip", None),
    )
    out_specs = P("view", "strip", None)
    return jax.shard_map(
        per_device, mesh=mesh, in_specs=in_specs, out_specs=out_specs, check_vma=False
    )
```

profile of v0, /device:TPU:12, one launch (start us, length us, event | category | flops | bytes accessed | tf_op | source)
XLA Modules:
  0.0 247.6 jit_solution(7047850341351948367)
XLA Ops:
  6.5 1.3 fusion.31
  7.9 1.9 fusion.32
  9.8 0.7 copy.80
  10.6 0.8 convert_reduce_fusion
  12.1 1.3 copy.70
  13.5 2.2 copy.71
  15.7 2.2 copy.72
  17.9 2.2 copy.73
  20.2 2.2 copy.74
  22.4 2.2 copy.75
  24.6 10.7 %concatenate.5 = bf16[1536,1920]{1,0:T(8,128)(2,1)} concatenate(bf16[1536,192]{1,0:T(8,128)(2,1)S(1)} %copy.70, bf16[1536,192]{1,0:T(8,128)(2,1)} %copy.71, bf16[1536,192]{1,0:T(8,128)(2,1)} %copy.72, bf16[1536,192]{1,0:T(8,128)(2,1)} %copy.73, bf16[1536,192]{1,0:T(8,128)(2,1)} %copy.74, bf16[1536,192]{1,0:T(8,128)(2,1)} %copy.75, bf16[1536,768]{1,0:T(8,128)(2,1)} %param.24), dimensions={1} | concatenate | bytes 11796480 | tf_op jit(solution)/shard_map/concatenate | solution.py:58
  35.9 21.9 %all-gather.2.cloned.1.call-done = bf16[1024,1536]{1,0:T(8,128)(2,1)} async-done(((bf16[128,1536]{1,0:T(8,128)(2,1)}), bf16[1024,1536]{1,0:T(8,128)(2,1)}) %all-gather.2.cloned.1.call-update) | async-done | bytes 3145744 | tf_op jit(solution)/shard_map/all_gather | solution.py:63
  57.7 11.9 %fusion.61 = (bf16[1024,1920]{1,0:T(8,128)(2,1)S(1)}, f32[1024,1920]{1,0:T(8,128)}) fusion(bf16[1024,1536]{1,0:T(8,128)(2,1)} %all-gather.2.cloned.1.call-done, bf16[1536,1920]{1,0:T(8,128)(2,1)} %concatenate.5), kind=kOutput, calls=%fused_computation.87 | convolution fusion | flops 6041763840 | bytes 20840448 | tf_op jit(solution)/shard_map/dot_general | solution.py:62
  69.7 1.9 fusion.59
  71.6 1.2 copy.78
  72.9 2.0 copy.77
  74.8 4.1 %gather_fusion = bf16[64,128,384]{2,1,0:T(8,128)(2,1)} fusion(bf16[8,128,384]{2,1,0:T(8,128)(2,1)S(1)} %bitcast.59, s32[1024]{0:T(1024)} %pad_clamp_fusion.1), kind=kCustom, calls=%fused_computation | custom fusion | bytes 12583168 | tf_op jit(solution)/shard_map/gather | solution.py:87
  79.0 7.4 %all-to-all-start = ((bf16[32,2,128,384]{3,2,1,0:T(8,128)(2,1)}), bf16[32,2,128,384]{3,2,1,0:T(8,128)(2,1)}, u32[]{:S(2)}, u32[]{:S(2)}) async-start(bf16[32,2,128,384]{3,2,1,0:T(8,128)(2,1)} %bitcast.60), calls=%async_computation.1 | async-start | bytes 12582912 | tf_op jit(solution)/shard_map/all_to_all | solution.py:88
  86.7 7.7 %fusion.22 = f32[1024,1536]{1,0:T(8,128)} fusion(bf16[768,1536]{1,0:T(8,128)(2,1)S(1)} %copy-done, f32[1024,1920]{1,0:T(8,128)} %get-tuple-element.14), kind=kOutput, calls=%fused_computation.30 | convolution fusion | flops 2422996992 | bytes 11796480 | tf_op jit(solution)/shard_map/dot_general | solution.py:32
  94.4 7.4 %fusion.67 = (f32[3,1024]{1,0:T(4,128)S(1)}, f32[3,1024,1024]{1,2,0:T(8,128)}) fusion(bf16[1024,3,64]{0,2,1:T(8,128)(2,1)S(1)} %bitcast.68, bf16[1024,3,64]{0,2,1:T(8,128)(2,1)S(1)} %bitcast.67), kind=kOutput, calls=%fused_computation.89 | convolution fusion | flops 412091392 | bytes 13381632 | tf_op jit(solution)/shard_map/sub | solution.py:24
  101.9 5.8 %fusion.29 = bf16[3,64,1024]{2,1,0:T(8,128)(2,1)S(1)} fusion(bf16[1024,3,64]{0,2,1:T(8,128)(2,1)S(1)} %bitcast.69, f32[3,1024,1024]{1,2,0:T(8,128)} %get-tuple-element.18, f32[3,1024]{1,0:T(4,128)S(1)} %get-tuple-element.17), kind=kOutput, calls=%fused_computation.36 | convolution fusion | flops 409141248 | bytes 13381632 | tf_op jit(solution)/shard_map/hqk,khe->qhe/dot_general | solution.py:25
  107.8 5.6 %add_convert_fusion = bf16[1024,1536]{1,0:T(8,128)(2,1)} fusion(f32[1024,1536]{1,0:T(8,128)} %fusion.22, bf16[1024,192]{0,1:T(8,128)(2,1)S(1)} %bitcast.66, bf16[192,1536]{1,0:T(8,128)(2,1)S(1)} %copy-done.5), kind=kOutput, calls=%fused_computation.11 | convolution fusion | flops 607125504 | bytes 10420224 | tf_op jit(solution)/shard_map/dot_general | solution.py:32
  115.0 44.2 %all-to-all-done = bf16[32,2,128,384]{3,2,1,0:T(8,128)(2,1)} async-done(((bf16[32,2,128,384]{3,2,1,0:T(8,128)(2,1)}), bf16[32,2,128,384]{3,2,1,0:T(8,128)(2,1)}, u32[]{:S(2)}, u32[]{:S(2)}) %all-to-all-start) | async-done | bytes 6291488 | tf_op jit(solution)/shard_map/all_to_all | solution.py:88
  159.2 6.1 %gather_fusion.1 = bf16[40,128,384]{2,1,0:T(8,128)(2,1)} fusion(bf16[64,128,384]{2,1,0:T(8,128)(2,1)} %bitcast.10, s32[1024]{0:T(1024)S(1)} %pad_clamp_fusion), kind=kCustom, calls=%fused_computation.1 | custom fusion | bytes 7864480 | tf_op jit(solution)/shard_map/gather | solution.py:101
  165.3 6.4 %fusion.60 = (bf16[8,640,192]{2,1,0:T(8,128)(2,1)}, bf16[8,640,192]{2,1,0:T(8,128)(2,1)}) fusion(bf16[8,640,384]{2,1,0:T(8,128)(2,1)} %bitcast.61), kind=kLoop, calls=%fused_computation.86 | loop fusion | bytes 7864320 | tf_op jit(solution)/shard_map/slice | solution.py:112
  171.6 3.0 %copy.88 = bf16[8,640,192]{1,2,0:T(8,128)(2,1)S(1)} copy(bf16[8,640,192]{2,1,0:T(8,128)(2,1)} %get-tuple-element.11) | data formatting | bytes 3932160 | tf_op jit(solution)/shard_map/slice | solution.py:112
  174.7 4.3 %copy.86 = bf16[8,640,192]{1,2,0:T(8,128)(2,1)} copy(bf16[8,640,192]{2,1,0:T(8,128)(2,1)} %get-tuple-element.12) | data formatting | bytes 3932160 | tf_op jit(solution)/shard_map/slice | solution.py:115
  179.0 4.8 %fusion.62 = (f32[8,3,128]{2,1,0:T(4,128)S(1)}, f32[8,3,128,640]{3,2,1,0:T(8,128)}) fusion(pred[8,640]{1,0:T(8,128)(4,1)S(1)} %broadcast_bitcast_fusion, bf16[8,640,3,64]{1,3,2,0:T(8,128)(2,1)S(1)} %bitcast.63, bf16[8,128,3,64]{1,0,3,2:T(8,128)(2,1)S(1)} %bitcast.70), kind=kOutput, calls=%fused_computation.88 | convolution fusion | flops 259523200 | bytes 10241024 | tf_op jit(solution)/shard_map/vmap()/sub | solution.py:24
  183.8 5.6 %fusion.30 = bf16[8,128,3,64]{1,3,2,0:T(8,128)(2,1)S(1)} fusion(bf16[8,640,3,64]{1,3,2,0:T(8,128)(2,1)} %bitcast.64, f32[8,3,128,640]{3,2,1,0:T(8,128)} %get-tuple-element.16, f32[8,3,128]{2,1,0:T(4,128)S(1)} %get-tuple-element.15), kind=kOutput, calls=%fused_computation.37 | convolution fusion | flops 255787008 | bytes 10235904 | tf_op jit(solution)/shard_map/vmap(hqk,khe->qhe)/dot_general | solution.py:25
  189.7 2.7 %convolution_convert_fusion = bf16[1024,1536]{1,0:T(8,128)(2,1)} fusion(bf16[192,1536]{1,0:T(8,128)(2,1)S(1)} %copy-done.6, bf16[24,8,8,128]{3,2,1,0:T(8,128)(2,1)S(1)} %bitcast.62), kind=kOutput, calls=%fused_computation.21 | convolution fusion | flops 605552640 | bytes 4128768 | tf_op jit(solution)/shard_map/dot_general | solution.py:32
  192.4 46.6 %reduce-scatter.5.cloned.1.call-done = bf16[128,1536]{1,0:T(8,128)(2,1)} async-done(((bf16[1024,1536]{1,0:T(8,128)(2,1)}), bf16[128,1536]{1,0:T(8,128)(2,1)}) %reduce-scatter.5.cloned.1.call-update) | async-done | bytes 393232 | tf_op jit(solution)/shard_map/reduce_scatter | solution.py:127
  239.0 2.0 fusion.36
  (48 shorter events, 3.7 us)
Async XLA Ops:
  6.5 80.1 %copy-start = (bf16[768,1536]{1,0:T(8,128)(2,1)S(1)}, bf16[768,1536]{1,0:T(8,128)(2,1)}, u32[]{:S(2)}) copy-start(bf16[768,1536]{1,0:T(8,128)(2,1)} %param.25) | copy-start | bytes 7077892
  6.5 51.2 %all-gather.2.cloned.1.call-start = ((), (), s32[]{:S(2)}) async-start(), calls=%async_computation.3 | async-start | bytes 3538944 | tf_op jit(solution)/shard_map/all_gather | solution.py:63
  11.4 0.6 copy-start.8
  79.0 80.2 %all-to-all-start = ((bf16[32,2,128,384]{3,2,1,0:T(8,128)(2,1)}), bf16[32,2,128,384]{3,2,1,0:T(8,128)(2,1)}, u32[]{:S(2)}, u32[]{:S(2)}) async-start(bf16[32,2,128,384]{3,2,1,0:T(8,128)(2,1)} %bitcast.60), calls=%async_computation.1 | async-start | bytes 12582912 | tf_op jit(solution)/shard_map/all_to_all | solution.py:88
  86.4 106.0 %reduce-scatter.3.cloned.1.call-start = ((), (), s32[]{:S(2)}) async-start(), calls=%async_computation.4 | async-start | bytes 3538944 | tf_op jit(solution)/shard_map/reduce_scatter | solution.py:121
  86.7 7.7 %copy-start.7 = (bf16[1024,192]{0,1:T(8,128)(2,1)S(1)}, bf16[1024,192]{0,1:T(8,128)(2,1)}, u32[]{:S(2)}) copy-start(bf16[1024,192]{0,1:T(8,128)(2,1)} %copy.77) | copy-start | bytes 1179652
  94.4 7.4 %copy-start.4 = (bf16[1024,192]{1,0:T(8,128)(2,1)S(1)}, bf16[1024,192]{1,0:T(8,128)(2,1)}, u32[]{:S(2)}) copy-start(bf16[1024,192]{1,0:T(8,128)(2,1)} %get-tuple-element.10) | copy-start | bytes 1179652
  101.9 5.9 %copy-start.5 = (bf16[192,1536]{1,0:T(8,128)(2,1)S(1)}, bf16[192,1536]{1,0:T(8,128)(2,1)}, u32[]{:S(2)}) copy-start(bf16[192,1536]{1,0:T(8,128)(2,1)} %param.19) | copy-start | bytes 1769476
  107.8 5.9 %copy-start.9 = (s32[32,8]{0,1:T(8,128)S(1)}, s32[32,8]{0,1:T(8,128)}, u32[]{:S(2)}) copy-start(s32[32,8]{0,1:T(8,128)} %param.15) | copy-start | bytes 3076
  107.8 6.9 %copy-start.3 = (bf16[1024,192]{1,0:T(8,128)(2,1)S(1)}, bf16[1024,192]{1,0:T(8,128)(2,1)}, u32[]{:S(2)}) copy-start(bf16[1024,192]{1,0:T(8,128)(2,1)} %get-tuple-element.8) | copy-start | bytes 1179652
  113.4 125.6 %reduce-scatter.5.cloned.1.call-start = ((), (), s32[]{:S(2)}) async-start(), calls=%async_computation.5 | async-start | bytes 3538944 | tf_op jit(solution)/shard_map/reduce_scatter | solution.py:127
  183.8 5.9 %copy-start.6 = (bf16[192,1536]{1,0:T(8,128)(2,1)S(1)}, bf16[192,1536]{1,0:T(8,128)(2,1)}, u32[]{:S(2)}) copy-start(bf16[192,1536]{1,0:T(8,128)(2,1)} %param.23) | copy-start | bytes 1769476
  189.7 49.4 %copy-start.2 = (bf16[1,128,1536]{2,1,0:T(8,128)(2,1)S(1)}, bf16[1,128,1536]{2,1,0:T(8,128)(2,1)}, u32[]{:S(2)}) copy-start(bf16[1,128,1536]{2,1,0:T(8,128)(2,1)} %param.13) | copy-start | bytes 1179652
  189.7 51.4 %copy-start.1 = (bf16[768,1536]{1,0:T(8,128)(2,1)S(1)}, bf16[768,1536]{1,0:T(8,128)(2,1)}, u32[]{:S(2)}) copy-start(bf16[768,1536]{1,0:T(8,128)(2,1)} %param.25) | copy-start | bytes 7077892
Sparse Core Ops, SparseCore 0:
  9.9 47.8 all-gather.1
  113.6 45.5 reduce-scatter.2
  192.5 46.4 reduce-scatter.4
where the time goes:
time: 249 us; the launch traced here: 248 us
  waiting for transfers between devices  113 us (45%)
  local copies, waits for them, and re-layouts  54.6 us (22%)
  matrix products  51.5 us (21%)
  between operations  13.3 us (5%)
  starting transfers between devices  7.93 us (3%)
  other arithmetic  7.46 us (3%)
    reduce_scatter x1, waiting for transfers between devices, per_device(): lax.psum_scatter(branch_term(cross_mix, cross_out).astype(jnp.bfloat16),...  46.6 us
    all_to_all x1, waiting for transfers between devices, per_device(): lax.all_to_all(outgoing, 'view', split_axis=0, concat_axis=0, tiled=True)  44.2 us
    all_gather x1, waiting for transfers between devices, per_device(): lax.all_gather(normed, 'strip', axis=0, tiled=True)  21.9 us
    dot_general x3, matrix products, branch_term(): return jnp.dot(mixed_rows, weight, preferred_element_type=jnp.float32)  16 us
    unnamed x28, local copies, waits for them, and re-layouts  13.7 us
    sub x2, matrix products, attend_heads(): weights = jax.nn.softmax(scores, axis=-1).astype(jnp.bfloat16)  12.1 us
    dot_general x1, matrix products, per_device(): jnp.dot(lax.all_gather(normed, 'strip', axis=0, tiled=True), stacked, pre...  11.9 us
    dot_general x2, matrix products, attend_heads(): jnp.einsum('hqk,khe->qhe', weights, value_heads, preferred_element_type=j...  11.4 us
  transfers between devices with their start and end apart: 4, of which 3 were waited for; matrix products, arithmetic and copies ran while one was open for 35% of the time, Pallas kernels for 0%

commit v1 on v0

--- a/solution.py
+++ b/solution.py
@@ -47,6 +47,18 @@
     mlp_up,
     mlp_down,
 ):
+
+    def see_grid_by_axis(field, a_name, array_axis):
+        return jnp.concatenate(
+            lax.all_to_all(
+                jnp.stack(tuple((field for _ in range(lax.psum(1, axis_name=a_name)))), axis=0),
+                axis_name=a_name,
+                split_axis=0,
+                concat_axis=0,
+            ),
+            array_axis,
+        )
+
     n_view = lax.axis_size("view")
     n_strip = lax.axis_size("strip")
     my_view = lax.axis_index("view")
@@ -60,9 +72,7 @@
     )
     split_at = 6 * head_cols
     product = jnp.dot(
-        lax.all_gather(normed, "strip", axis=0, tiled=True),
-        stacked,
-        preferred_element_type=jnp.float32,
+        see_grid_by_axis(normed, "strip", 0), stacked, preferred_element_type=jnp.float32
     )
     projected = jnp.concatenate(
         [product[:, :split_at], jax.nn.gelu(product[:, split_at:])], 1

time: 249 us -> 282 us (1.13)
  waiting for transfers between devices: 113 us -> 137 us
  starting transfers between devices: 7.93 us -> 16.6 us
    all_to_all x0 -> x1, waiting for transfers between devices: none -> 48.5 us  [see_grid_by_axis(): lax.all_to_all(jnp.stack(tuple((field for _ in range(lax.psum(1, axis_nam...]
    all_gather x1 -> x0, waiting for transfers between devices: 21.9 us -> none  [per_device(): lax.all_gather(normed, 'strip', axis=0, tiled=True)]
    all_to_all x0 -> x1, starting transfers between devices: none -> 8.6 us  [see_grid_by_axis(): lax.all_to_all(jnp.stack(tuple((field for _ in range(lax.psum(1, axis_nam...]
    unnamed x28 -> x30, local copies, waits for them, and re-layouts: 13.7 us -> 13 us
  transfers between devices with their start and end apart: 4 -> 4, of which waited for: 3 -> 3; matrix products, arithmetic and copies ran while one was open for 35% -> 31% of each run, Pallas kernels for 0% -> 0%
where the time goes in v1:
time: 282 us; the launch traced here: 281 us
  waiting for transfers between devices  137 us (49%)
  local copies, waits for them, and re-layouts  55.8 us (20%)
  matrix products  51.5 us (18%)
  starting transfers between devices  16.6 us (6%)
  between operations  13.6 us (5%)
  other arithmetic  6.72 us (2%)
    all_to_all x1, waiting for transfers between devices, see_grid_by_axis(): lax.all_to_all(jnp.stack(tuple((field for _ in range(lax.psum(1, axis_nam...  48.5 us
    all_to_all x1, waiting for transfers between devices, per_device(): lax.all_to_all(outgoing, 'view', split_axis=0, concat_axis=0, tiled=True)  44.2 us
    reduce_scatter x1, waiting for transfers between devices, per_device(): lax.psum_scatter(branch_term(cross_mix, cross_out).astype(jnp.bfloat16),...  44 us
    dot_general x3, matrix products, branch_term(): return jnp.dot(mixed_rows, weight, preferred_element_type=jnp.float32)  16 us
    unnamed x30, local copies, waits for them, and re-layouts  13 us
    sub x2, matrix products, attend_heads(): weights = jax.nn.softmax(scores, axis=-1).astype(jnp.bfloat16)  12.1 us
    dot_general x1, matrix products, per_device(): jnp.dot(see_grid_by_axis(normed, 'strip', 0), stacked, preferred_element_...  11.9 us
    dot_general x2, matrix products, attend_heads(): jnp.einsum('hqk,khe->qhe', weights, value_heads, preferred_element_type=j...  11.4 us
  transfers between devices with their start and end apart: 4, of which 3 were waited for; matrix products, arithmetic and copies ran while one was open for 31% of the time, Pallas kernels for 0%

profile of v1, /device:TPU:12, one launch (start us, length us, event | category | flops | bytes accessed | tf_op | source)
XLA Modules:
  0.0 281.1 jit_solution(16683540514891628597)
XLA Ops:
  6.5 1.3 fusion.33
  7.9 1.1 fusion.38
  9.0 1.9 stack.5
  10.9 8.6 %all-to-all-start = ((bf16[8,128,1536]{2,1,0:T(8,128)(2,1)}), bf16[8,128,1536]{2,1,0:T(8,128)(2,1)}, u32[]{:S(2)}, u32[]{:S(2)}) async-start(bf16[8,128,1536]{2,1,0:T(8,128)(2,1)} %stack.5), calls=%async_computation | async-start | bytes 6291456 | tf_op jit(solution)/shard_map/all_to_all | solution.py:53
  21.2 1.3 copy.70
  22.5 2.2 copy.71
  24.7 2.2 copy.72
  27.0 2.2 copy.73
  29.2 2.3 copy.74
  31.5 2.2 copy.75
  33.7 10.6 %concatenate.5 = bf16[1536,1920]{1,0:T(8,128)(2,1)} concatenate(bf16[1536,192]{1,0:T(8,128)(2,1)S(1)} %copy.70, bf16[1536,192]{1,0:T(8,128)(2,1)} %copy.71, bf16[1536,192]{1,0:T(8,128)(2,1)} %copy.72, bf16[1536,192]{1,0:T(8,128)(2,1)} %copy.73, bf16[1536,192]{1,0:T(8,128)(2,1)} %copy.74, bf16[1536,192]{1,0:T(8,128)(2,1)} %copy.75, bf16[1536,768]{1,0:T(8,128)(2,1)} %param.24), dimensions={1} | concatenate | bytes 11796480 | tf_op jit(solution)/shard_map/concatenate | solution.py:70
  44.9 48.5 %all-to-all-done = bf16[8,128,1536]{2,1,0:T(8,128)(2,1)} async-done(((bf16[8,128,1536]{2,1,0:T(8,128)(2,1)}), bf16[8,128,1536]{2,1,0:T(8,128)(2,1)}, u32[]{:S(2)}, u32[]{:S(2)}) %all-to-all-start) | async-done | bytes 3145760 | tf_op jit(solution)/shard_map/all_to_all | solution.py:53
  93.4 11.9 %fusion.64 = (bf16[1024,1920]{1,0:T(8,128)(2,1)S(1)}, f32[1024,1920]{1,0:T(8,128)}) fusion(bf16[1024,1536]{1,0:T(8,128)(2,1)} %bitcast.2, bf16[1536,1920]{1,0:T(8,128)(2,1)} %concatenate.5), kind=kOutput, calls=%fused_computation.89 | convolution fusion | flops 6041763840 | bytes 20840448 | tf_op jit(solution)/shard_map/dot_general | solution.py:74
  105.4 1.9 fusion.62
  107.3 1.2 copy.78
  108.5 2.0 copy.77
  110.5 4.1 %gather_fusion = bf16[64,128,384]{2,1,0:T(8,128)(2,1)} fusion(bf16[8,128,384]{2,1,0:T(8,128)(2,1)S(1)} %bitcast.69, s32[1024]{0:T(1024)} %pad_clamp_fusion.1), kind=kCustom, calls=%fused_computation | custom fusion | bytes 12583168 | tf_op jit(solution)/shard_map/gather | solution.py:97
  114.6 7.5 %all-to-all-start.1 = ((bf16[32,2,128,384]{3,2,1,0:T(8,128)(2,1)}), bf16[32,2,128,384]{3,2,1,0:T(8,128)(2,1)}, u32[]{:S(2)}, u32[]{:S(2)}) async-start(bf16[32,2,128,384]{3,2,1,0:T(8,128)(2,1)} %bitcast.70), calls=%async_computation.2 | async-start | bytes 12582912 | tf_op jit(solution)/shard_map/all_to_all | solution.py:98
  122.4 7.7 %fusion.22 = f32[1024,1536]{1,0:T(8,128)} fusion(bf16[768,1536]{1,0:T(8,128)(2,1)S(1)} %copy-done, f32[1024,1920]{1,0:T(8,128)} %get-tuple-element.14), kind=kOutput, calls=%fused_computation.30 | convolution fusion | flops 2422996992 | bytes 11796480 | tf_op jit(solution)/shard_map/dot_general | solution.py:32
  130.1 7.4 %fusion.70 = (f32[3,1024]{1,0:T(4,128)S(1)}, f32[3,1024,1024]{1,2,0:T(8,128)}) fusion(bf16[1024,3,64]{0,2,1:T(8,128)(2,1)S(1)} %bitcast.78, bf16[1024,3,64]{0,2,1:T(8,128)(2,1)S(1)} %bitcast.77), kind=kOutput, calls=%fused_computation.91 | convolution fusion | flops 412091392 | bytes 13381632 | tf_op jit(solution)/shard_map/sub | solution.py:24
  137.7 5.8 %fusion.29 = bf16[3,64,1024]{2,1,0:T(8,128)(2,1)S(1)} fusion(bf16[1024,3,64]{0,2,1:T(8,128)(2,1)S(1)} %bitcast.79, f32[3,1024,1024]{1,2,0:T(8,128)} %get-tuple-element.18, f32[3,1024]{1,0:T(4,128)S(1)} %get-tuple-element.17), kind=kOutput, calls=%fused_computation.36 | convolution fusion | flops 409141248 | bytes 13381632 | tf_op jit(solution)/shard_map/hqk,khe->qhe/dot_general | solution.py:25
  143.6 5.6 %add_convert_fusion = bf16[1024,1536]{1,0:T(8,128)(2,1)} fusion(f32[1024,1536]{1,0:T(8,128)} %fusion.22, bf16[1024,192]{0,1:T(8,128)(2,1)S(1)} %bitcast.76, bf16[192,1536]{1,0:T(8,128)(2,1)S(1)} %copy-done.5), kind=kOutput, calls=%fused_computation.11 | convolution fusion | flops 607125504 | bytes 10420224 | tf_op jit(solution)/shard_map/dot_general | solution.py:32
  150.7 44.2 %all-to-all-done.1 = bf16[32,2,128,384]{3,2,1,0:T(8,128)(2,1)} async-done(((bf16[32,2,128,384]{3,2,1,0:T(8,128)(2,1)}), bf16[32,2,128,384]{3,2,1,0:T(8,128)(2,1)}, u32[]{:S(2)}, u32[]{:S(2)}) %all-to-all-start.1) | async-done | bytes 6291488 | tf_op jit(solution)/shard_map/all_to_all | solution.py:98
  195.0 6.1 %gather_fusion.1 = bf16[40,128,384]{2,1,0:T(8,128)(2,1)} fusion(bf16[64,128,384]{2,1,0:T(8,128)(2,1)} %bitcast.11, s32[1024]{0:T(1024)S(1)} %pad_clamp_fusion), kind=kCustom, calls=%fused_computation.1 | custom fusion | bytes 7864480 | tf_op jit(solution)/shard_map/gather | solution.py:111
  201.0 6.4 %fusion.63 = (bf16[8,640,192]{2,1,0:T(8,128)(2,1)}, bf16[8,640,192]{2,1,0:T(8,128)(2,1)}) fusion(bf16[8,640,384]{2,1,0:T(8,128)(2,1)} %bitcast.71), kind=kLoop, calls=%fused_computation.88 | loop fusion | bytes 7864320 | tf_op jit(solution)/shard_map/slice | solution.py:122
  207.4 3.0 %copy.88 = bf16[8,640,192]{1,2,0:T(8,128)(2,1)S(1)} copy(bf16[8,640,192]{2,1,0:T(8,128)(2,1)} %get-tuple-element.11) | data formatting | bytes 3932160 | tf_op jit(solution)/shard_map/slice | solution.py:122
  210.5 4.3 %copy.86 = bf16[8,640,192]{1,2,0:T(8,128)(2,1)} copy(bf16[8,640,192]{2,1,0:T(8,128)(2,1)} %get-tuple-element.12) | data formatting | bytes 3932160 | tf_op jit(solution)/shard_map/slice | solution.py:125
  214.7 4.8 %fusion.65 = (f32[8,3,128]{2,1,0:T(4,128)S(1)}, f32[8,3,128,640]{3,2,1,0:T(8,128)}) fusion(pred[8,640]{1,0:T(8,128)(4,1)S(1)} %broadcast_bitcast_fusion, bf16[8,640,3,64]{1,3,2,0:T(8,128)(2,1)S(1)} %bitcast.73, bf16[8,128,3,64]{1,0,3,2:T(8,128)(2,1)S(1)} %bitcast.80), kind=kOutput, calls=%fused_computation.90 | convolution fusion | flops 259523200 | bytes 10241024 | tf_op jit(solution)/shard_map/vmap()/sub | solution.py:24
  219.5 5.6 %fusion.30 = bf16[8,128,3,64]{1,3,2,0:T(8,128)(2,1)S(1)} fusion(bf16[8,640,3,64]{1,3,2,0:T(8,128)(2,1)} %bitcast.74, f32[8,3,128,640]{3,2,1,0:T(8,128)} %get-tuple-element.16, f32[8,3,128]{2,1,0:T(4,128)S(1)} %get-tuple-element.15), kind=kOutput, calls=%fused_computation.37 | convolution fusion | flops 255787008 | bytes 10235904 | tf_op jit(solution)/shard_map/vmap(hqk,khe->qhe)/dot_general | solution.py:25
  225.4 2.7 convolution_convert_fusion
  228.2 44.0 %reduce-scatter.5.cloned.1.call-done = bf16[128,1536]{1,0:T(8,128)(2,1)} async-done(((bf16[1024,1536]{1,0:T(8,128)(2,1)}), bf16[128,1536]{1,0:T(8,128)(2,1)}) %reduce-scatter.5.cloned.1.call-update) | async-done | bytes 393232 | tf_op jit(solution)/shard_map/reduce_scatter | solution.py:137
  272.2 2.0 fusion.39
  (50 shorter events, 4.5 us)
Async XLA Ops:
  6.5 115.9 %copy-start = (bf16[768,1536]{1,0:T(8,128)(2,1)S(1)}, bf16[768,1536]{1,0:T(8,128)(2,1)}, u32[]{:S(2)}) copy-start(bf16[768,1536]{1,0:T(8,128)(2,1)} %param.25) | copy-start | bytes 7077892
  10.9 8.6 %copy-start.9 = (s32[32,8,5]{0,1,2:T(8,128)S(1)}, s32[32,8,5]{0,1,2:T(8,128)}, u32[]{:S(2)}) copy-start(s32[32,8,5]{0,1,2:T(8,128)} %param.14) | copy-start | bytes 15364
  10.9 82.5 %all-to-all-start = ((bf16[8,128,1536]{2,1,0:T(8,128)(2,1)}), bf16[8,128,1536]{2,1,0:T(8,128)(2,1)}, u32[]{:S(2)}, u32[]{:S(2)}) async-start(bf16[8,128,1536]{2,1,0:T(8,128)(2,1)} %stack.5), calls=%async_computation | async-start | bytes 6291456 | tf_op jit(solution)/shard_map/all_to_all | solution.py:53
  20.5 0.6 copy-start.8
  114.6 80.3 %all-to-all-start.1 = ((bf16[32,2,128,384]{3,2,1,0:T(8,128)(2,1)}), bf16[32,2,128,384]{3,2,1,0:T(8,128)(2,1)}, u32[]{:S(2)}, u32[]{:S(2)}) async-start(bf16[32,2,128,384]{3,2,1,0:T(8,128)(2,1)} %bitcast.70), calls=%async_computation.2 | async-start | bytes 12582912 | tf_op jit(solution)/shard_map/all_to_all | solution.py:98
  122.2 106.0 %reduce-scatter.3.cloned.1.call-start = ((), (), s32[]{:S(2)}) async-start(), calls=%async_computation.4 | async-start | bytes 3538944 | tf_op jit(solution)/shard_map/reduce_scatter | solution.py:131
  122.4 7.7 %copy-start.7 = (bf16[1024,192]{0,1:T(8,128)(2,1)S(1)}, bf16[1024,192]{0,1:T(8,128)(2,1)}, u32[]{:S(2)}) copy-start(bf16[1024,192]{0,1:T(8,128)(2,1)} %copy.77) | copy-start | bytes 1179652
  130.1 7.4 %copy-start.4 = (bf16[1024,192]{1,0:T(8,128)(2,1)S(1)}, bf16[1024,192]{1,0:T(8,128)(2,1)}, u32[]{:S(2)}) copy-start(bf16[1024,192]{1,0:T(8,128)(2,1)} %get-tuple-element.10) | copy-start | bytes 1179652
  137.7 5.9 %copy-start.5 = (bf16[192,1536]{1,0:T(8,128)(2,1)S(1)}, bf16[192,1536]{1,0:T(8,128)(2,1)}, u32[]{:S(2)}) copy-start(bf16[192,1536]{1,0:T(8,128)(2,1)} %param.19) | copy-start | bytes 1769476
  143.6 5.9 %copy-start.10 = (s32[32,8]{0,1:T(8,128)S(1)}, s32[32,8]{0,1:T(8,128)}, u32[]{:S(2)}) copy-start(s32[32,8]{0,1:T(8,128)} %param.15) | copy-start | bytes 3076
  143.6 6.9 %copy-start.3 = (bf16[1024,192]{1,0:T(8,128)(2,1)S(1)}, bf16[1024,192]{1,0:T(8,128)(2,1)}, u32[]{:S(2)}) copy-start(bf16[1024,192]{1,0:T(8,128)(2,1)} %get-tuple-element.8) | copy-start | bytes 1179652
  149.2 123.0 %reduce-scatter.5.cloned.1.call-start = ((), (), s32[]{:S(2)}) async-start(), calls=%async_computation.5 | async-start | bytes 3538944 | tf_op jit(solution)/shard_map/reduce_scatter | solution.py:137
  219.5 5.9 %copy-start.6 = (bf16[192,1536]{1,0:T(8,128)(2,1)S(1)}, bf16[192,1536]{1,0:T(8,128)(2,1)}, u32[]{:S(2)}) copy-start(bf16[192,1536]{1,0:T(8,128)(2,1)} %param.23) | copy-start | bytes 1769476
  225.4 46.8 %copy-start.2 = (bf16[1,128,1536]{2,1,0:T(8,128)(2,1)S(1)}, bf16[1,128,1536]{2,1,0:T(8,128)(2,1)}, u32[]{:S(2)}) copy-start(bf16[1,128,1536]{2,1,0:T(8,128)(2,1)} %param.13) | copy-start | bytes 1179652
  225.4 48.8 %copy-start.1 = (bf16[768,1536]{1,0:T(8,128)(2,1)S(1)}, bf16[768,1536]{1,0:T(8,128)(2,1)}, u32[]{:S(2)}) copy-start(bf16[768,1536]{1,0:T(8,128)(2,1)} %param.25) | copy-start | bytes 7077892
Sparse Core Ops, SparseCore 0:
  149.3 43.2 reduce-scatter.2
  228.3 43.9 reduce-scatter.4
